TPU v7x, 32 devices: a whole 2x2x4 slice. The times are simulated.
32 devices in a mesh: gx: 8 (over z, core), gy: 4 (over y, x).
Axes of the slice: x: 2, y: 2, z: 4, core: 2. Of those that a mesh axis runs over, the one named last changes fastest.
Arguments:
- signal: float32 [32768, 128], P(('gx', 'gy')), may hold values from -6 to 6
- filter_taps: float32 [32768, 128], P(('gx', 'gy')), may hold values from -6 to 6
- grad_out: float32 [32768, 128], P(('gx', 'gy')), may hold values from -0.03125 to 0.03125
Outputs:
- grad_signal: float32 [32768, 128], P(('gx', 'gy'))
- grad_filter: float32 [32768, 128], P(('gx', 'gy'))
All inputs are finite; a program needn't handle non-finite values.
Results may differ from a plain program's by a relative error of at most 0.000098.
Values sent between devices are 32-bit elements; how exact they have to be, the bound alone decides.
A program may use at most 128 MiB of HBM per device.

v0:
```python
import math

import jax
import jax.numpy as jnp
import numpy as np
from jax import lax
from jax.experimental import pallas as pl
from jax.experimental.pallas import tpu as pltpu
from jax.sharding import PartitionSpec as P

LANES = 128
f32, bf16 = jnp.float32, jnp.bfloat16


def halves(table):
    high = table.astype(np.float32).astype(bf16)
    low = (table - high.astype(np.float64)).astype(np.float32).astype(bf16)
    return np.stack([high, low])


def make_tables(rows):
    first = 2 * rows
    period = first * LANES
    low = np.arange(rows)
    angle = 2.0 * math.pi / first * (low[:, None] * low[None, :] % first)
    outer = np.concatenate([np.cos(angle), np.sin(angle)], axis=0)
    lane = np.arange(LANES)
    angle = 2.0 * math.pi / LANES * (lane[:, None] * lane[None, :] % LANES)
    c, s = np.cos(angle), np.sin(angle)
    inner = np.concatenate(
        [np.concatenate([c, s], axis=1), np.concatenate([-s, c], axis=1)], axis=0
    )
    angle = 2.0 * math.pi / period * (np.arange(first)[:, None] * lane[None, :] % period)
    turn = np.stack([np.cos(angle), np.sin(angle)]).astype(np.float32)
    return halves(outer), halves(inner), turn


def split(value):
    high = value.astype(bf16)
    return high, (value - high.astype(f32)).astype(bf16)


def mm(a, b):
    return jnp.dot(a, b, preferred_element_type=f32)


def left_product(outer_ref, high_ref, low_ref, out_ref, width):
    total = outer_ref.shape[1]
    block = min(total, 512)

    def step(rows):
        high = high_ref[:, :width]
        low = low_ref[:, :width]
        out_ref[rows, :width] = (
            mm(outer_ref[0, rows, :], high)
            + mm(outer_ref[0, rows, :], low)
            + mm(outer_ref[1, rows, :], high)
        )

    if block == total:
        step(slice(None))
    else:

        @pl.loop(0, total // block)
        def _(i):
            step(pl.ds(pl.multiple_of(i * block, block), block))


def right_product(value, inner_ref):
    high, low = split(value)
    return mm(high, inner_ref[0]) + mm(low, inner_ref[0]) + mm(high, inner_ref[1])


def correlate(load, store, rows, outer_ref, inner_ref, turn_ref, high_ref, low_ref, prod_ref):
    odd = lax.broadcasted_iota(jnp.int32, (rows, LANES), 0) % 2 == 1
    for q in range(3):
        high, low = split(load(q))
        high32, low32 = high.astype(f32), low.astype(f32)
        at = slice(q * LANES, (q + 1) * LANES)
        high_ref[:, at], low_ref[:, at] = high, low
        at = slice((q + 3) * LANES, (q + 4) * LANES)
        high_ref[:, at] = jnp.where(odd, -high32, high32).astype(bf16)
        low_ref[:, at] = jnp.where(odd, -low32, low32).astype(bf16)
    left_product(outer_ref, high_ref, low_ref, prod_ref, 6 * LANES)
    for h in range(2):

        def part(which, q):
            at = (q + 3 * h) * LANES
            return prod_ref[which * rows : (which + 1) * rows, at : at + LANES]

        cosine = turn_ref[0, h * rows : (h + 1) * rows, :]
        sine = turn_ref[1, h * rows : (h + 1) * rows, :]

        def rotate(real, imaginary):
            return jnp.concatenate(
                [real * cosine - imaginary * sine, real * sine + imaginary * cosine], axis=1
            )

        z = rotate(part(0, 0) - part(1, 1), part(1, 0) + part(0, 1))
        g = rotate(part(0, 2), part(1, 2))
        z = right_product(z, inner_ref)
        g = right_product(g, inner_ref)
        zr, zi, gr, gi = z[:, :LANES], z[:, LANES:], g[:, :LANES], g[:, LANES:]
        y = jnp.concatenate([zr * gr + zi * gi, zi * gr - zr * gi], axis=1)
        y = right_product(y, inner_ref)
        y = rotate(y[:, :LANES], y[:, LANES:])
        high, low = split(y)
        at = slice(2 * h * LANES, 2 * (h + 1) * LANES)
        high_ref[:, at], low_ref[:, at] = high, low
    left_product(outer_ref, high_ref, low_ref, prod_ref, 4 * LANES)
    scale = 1.0 / (2 * rows * LANES)

    def part(which, q):
        return prod_ref[which * rows : (which + 1) * rows, q * LANES : (q + 1) * LANES]

    real = [part(0, 2 * h) - part(1, 2 * h + 1) for h in range(2)]
    imaginary = [part(1, 2 * h) + part(0, 2 * h + 1) for h in range(2)]
    store(0, (real[0] + jnp.where(odd, -real[1], real[1])) * scale)
    store(1, (imaginary[0] + jnp.where(odd, -imaginary[1], imaginary[1])) * scale)


def local_kernel(x_ref, outer_ref, inner_ref, turn_ref, out_ref, high_ref, low_ref, prod_ref):
    rows = x_ref.shape[2]

    @pl.loop(0, x_ref.shape[1])
    def _(c):
        def store(q, value):
            out_ref[q, c] = value

        correlate(
            lambda q: x_ref[q, c],
            store,
            rows,
            outer_ref,
            inner_ref,
            turn_ref,
            high_ref,
            low_ref,
            prod_ref,
        )


def shards(signal, filter_taps, grad_out):
    rows_local, channels = signal.shape
    devices = lax.axis_size("gx") * lax.axis_size("gy")
    tiles = rows_local // LANES
    rows = devices * tiles
    own = channels // devices
    outer, inner, turn = make_tables(rows)
    x = jnp.stack([filter_taps, signal, grad_out])
    x = x.reshape(3, tiles, LANES, channels).transpose(0, 3, 1, 2)
    x = lax.all_to_all(x, ("gx", "gy"), split_axis=1, concat_axis=2, tiled=True)
    vmem = pl.BlockSpec(memory_space=pltpu.VMEM)
    y = pl.pallas_call(
        local_kernel,
        out_shape=jax.ShapeDtypeStruct((2, own, rows, LANES), f32),
        in_specs=[vmem] * 4,
        out_specs=vmem,
        scratch_shapes=[
            pltpu.VMEM((rows, 6 * LANES), bf16),
            pltpu.VMEM((rows, 6 * LANES), bf16),
            pltpu.VMEM((2 * rows, 6 * LANES), f32),
        ],
        compiler_params=pltpu.CompilerParams(vmem_limit_bytes=60 << 20),
    )(x, outer, inner, turn)
    y = lax.all_to_all(y, ("gx", "gy"), split_axis=2, concat_axis=1, tiled=True)
    y = y.transpose(0, 2, 3, 1).reshape(2, rows_local, channels)
    return y[0], y[1]


def solution(mesh):
    spec = P(("gx", "gy"), None)
    return jax.shard_map(
        shards, mesh=mesh, in_specs=(spec,) * 3, out_specs=(spec,) * 2, check_vma=False
    )
```

profile of v0, /device:TPU:0, one launch (start us, length us, event | category | flops | bytes accessed | tf_op | source)
XLA Modules:
  0.0 97.4 jit_solution(11267419968450862646)
XLA Ops:
  0.6 0.0 copy-start
  0.6 1.3 %copy.34 = f32[1,8,128,128]{2,1,0,3:T(8,128)S(1)} copy(f32[1,8,128,128]{3,2,1,0:T(8,128)} %bitcast.25) | data formatting | bytes 1048576 | tf_op jit(solution)/shard_map/stack | solution.py:150
  2.0 1.3 %copy.33 = f32[1,8,128,128]{2,1,0,3:T(8,128)S(1)} copy(f32[1,8,128,128]{3,2,1,0:T(8,128)} %bitcast.26) | data formatting | bytes 1048576 | tf_op jit(solution)/shard_map/stack | solution.py:150
  3.3 0.0 copy-done
  3.3 0.2 copy.35
  3.5 0.1 maximum_bitcast_fusion
  3.6 45.9 %all_to_all.36 = f32[3,128,8,128]{3,2,0,1:T(8,128)S(1)} all-to-all(f32[3,128,8,128]{3,2,0,1:T(8,128)S(1)} %maximum_bitcast_fusion), channel_id=1, replica_groups=mesh['gx'=8,'gy'=4] {'gx','gy'}, dimensions={1} | all-to-all | bytes 3145728 | tf_op jit(solution)/shard_map/all_to_all | solution.py:152
  49.5 1.3 %copy.41 = f32[3,4,32,8,128]{4,3,2,1,0:T(8,128)} copy(f32[3,4,32,8,128]{4,3,0,1,2:T(8,128)S(1)} %bitcast.21) | data formatting | bytes 3145728 | tf_op jit(solution)/shard_map/all_to_all | solution.py:152
  50.8 13.6 %shard_map.77 = f32[2,4,256,128]{3,2,1,0:T(8,128)} custom-call(f32[3,4,256,128]{3,2,1,0:T(8,128)} %bitcast.22, bf16[2,512,256]{2,1,0:T(8,128)(2,1)} %constant.6.clone.outer_ref, bf16[2,256,256]{2,1,0:T(8,128)(2,1)} %constant.7.clone.inner_ref, f32[2,512,128]{2,1,0:T(8,128)} %constant.8.clone.turn_ref), custom_call_target="tpu_custom_call" | custom-call | tf_op jit(solution)/shard_map/pallas_call | solution.py:154
  64.4 1.9 %copy.28 = f32[2,4,256,128]{3,1,0,2:T(4,128)S(1)} copy(f32[2,4,256,128]{3,2,1,0:T(8,128)} %shard_map.77) | data formatting | bytes 2097152 | tf_op jit(solution)/shard_map/pallas_call | solution.py:154
  66.3 28.6 %all_to_all.37 = f32[2,4,256,128]{3,1,0,2:T(4,128)S(1)} all-to-all(f32[2,4,256,128]{3,1,0,2:T(4,128)S(1)} %copy.28), channel_id=1, replica_groups=mesh['gx'=8,'gy'=4] {'gx','gy'}, dimensions={2} | all-to-all | bytes 2097152 | tf_op jit(solution)/shard_map/all_to_all | solution.py:166
  94.9 0.2 copy.42
  95.1 0.1 copy.30
  95.2 0.1 fusion
  95.3 1.0 %copy.38 = f32[1,8,128,128]{3,2,1,0:T(8,128)} copy(f32[1,8,128,128]{2,1,3,0:T(8,128)S(1)} %get-tuple-element.8) | data formatting | bytes 1048576
  96.4 1.0 %copy.37 = f32[1,8,128,128]{3,2,1,0:T(8,128)} copy(f32[1,8,128,128]{2,1,3,0:T(8,128)S(1)} %get-tuple-element.9) | data formatting | bytes 1048576
Async XLA Ops:
  0.6 2.6 %copy-start = (f32[1024,128]{1,0:T(8,128)S(1)}, f32[1024,128]{1,0:T(8,128)}, u32[]{:S(2)}) copy-start(f32[1024,128]{1,0:T(8,128)} %param.8) | copy-start | bytes 1572868
where the time goes:
time: 97.7 us; the launch traced here: 97.4 us
  blocking collectives  74.5 us (76%)
  Pallas kernels  13.6 us (14%)
  local copies, waits for them, and re-layouts  8.5 us (9%)
    all_to_all x1, blocking collectives, shards(): x = lax.all_to_all(x, ('gx', 'gy'), split_axis=1, concat_axis=2, tiled=True)  45.9 us
    all_to_all x1, blocking collectives, shards(): y = lax.all_to_all(y, ('gx', 'gy'), split_axis=2, concat_axis=1, tiled=True)  28.6 us
    pallas_call x1, Pallas kernels, shards(): pl.pallas_call(local_kernel, out_shape=jax.ShapeDtypeStruct((2, own, rows...  13.6 us
    another operation x3, local copies, waits for them, and re-layouts, shards(): x = jnp.stack([filter_taps, signal, grad_out])  2.84 us
    unnamed x4, local copies, waits for them, and re-layouts  2.07 us

commit v1 on v0

--- a/solution.py
+++ b/solution.py
@@ -1,3 +1,4 @@
+import functools
 import math
 
 import jax
@@ -119,53 +120,182 @@
     store(1, (imaginary[0] + jnp.where(odd, -imaginary[1], imaginary[1])) * scale)
 
 
-def local_kernel(x_ref, outer_ref, inner_ref, turn_ref, out_ref, high_ref, low_ref, prod_ref):
-    rows = x_ref.shape[2]
-
-    @pl.loop(0, x_ref.shape[1])
+def peer_of(me, offset, devices):
+    if devices & (devices - 1):
+        return (me + offset) % devices
+    peer = me
+    bit = 1
+    while bit < devices:
+        peer = peer + (offset // bit % 2) * (1 - 2 * (me // bit % 2)) * bit
+        bit *= 2
+    return peer
+
+
+def kernel(
+    columns,
+    signal_ref,
+    filter_ref,
+    grad_ref,
+    outer_hbm,
+    inner_hbm,
+    turn_hbm,
+    out0_ref,
+    out1_ref,
+    send,
+    recv,
+    back,
+    land,
+    outer_ref,
+    inner_ref,
+    turn_ref,
+    high_ref,
+    low_ref,
+    prod_ref,
+    table_sem,
+    send_sem,
+    recv_sem,
+    back_sem,
+    land_sem,
+):
+    own, devices, height, _ = recv.shape
+    tiles = height // 3
+    rows = devices * tiles
+    me = lax.axis_index("gx") * columns + lax.axis_index("gy")
+
+    def device(peer):
+        return (peer // columns, peer % columns)
+
+    def partner(i):
+        return peer_of(me, devices - 1 - i, devices)
+
+    barrier = pltpu.get_barrier_semaphore()
+
+    @pl.loop(0, devices - 1)
+    def _(i):
+        pl.semaphore_signal(
+            barrier, inc=1, device_id=device(partner(i)), device_id_type=pl.DeviceIdType.MESH
+        )
+
+    tables = [
+        pltpu.make_async_copy(a, b, table_sem.at[n])
+        for n, (a, b) in enumerate(
+            ((outer_hbm, outer_ref), (inner_hbm, inner_ref), (turn_hbm, turn_ref))
+        )
+    ]
+    for copy in tables:
+        copy.start()
+    for q, ref in enumerate((filter_ref, signal_ref, grad_ref)):
+        for j in range(tiles):
+            block = ref[j * LANES : (j + 1) * LANES, :].T
+            send[pl.ds(q * tiles + j, own * devices, stride=3 * tiles), :] = block
+    pl.semaphore_wait(barrier, devices - 1)
+
+    def outgoing(c, peer):
+        at = pl.multiple_of((peer * own + c) * 3 * tiles, 3 * tiles)
+        return pltpu.make_async_remote_copy(
+            src_ref=send.at[pl.ds(at, 3 * tiles), :],
+            dst_ref=recv.at[c, me],
+            send_sem=send_sem,
+            recv_sem=recv_sem.at[c],
+            device_id=device(peer),
+            device_id_type=pl.DeviceIdType.MESH,
+        )
+
+    def returning(c, peer):
+        at = pl.multiple_of((me * own + c) * 2 * tiles, 2 * tiles)
+        return pltpu.make_async_remote_copy(
+            src_ref=back.at[c, peer],
+            dst_ref=land.at[pl.ds(at, 2 * tiles), :],
+            send_sem=back_sem,
+            recv_sem=land_sem,
+            device_id=device(peer),
+            device_id_type=pl.DeviceIdType.MESH,
+        )
+
+    @pl.loop(0, own)
     def _(c):
+        @pl.loop(0, devices - 1)
+        def _(i):
+            outgoing(c, partner(i)).start()
+
+    @pl.loop(0, own)
+    def _(c):
+        at = pl.multiple_of((me * own + c) * 3 * tiles, 3 * tiles)
+        recv[c, me] = send[pl.ds(at, 3 * tiles), :]
+
+    for copy in tables:
+        copy.wait()
+
+    @pl.loop(0, own)
+    def _(c):
+        arrived = recv.at[c, pl.ds(0, devices - 1)]
+        pltpu.make_async_copy(arrived, arrived, recv_sem.at[c]).wait()
+
+        def load(q):
+            return recv[c, :, q * tiles : (q + 1) * tiles, :].reshape(rows, LANES)
+
         def store(q, value):
-            out_ref[q, c] = value
+            back[c, :, q * tiles : (q + 1) * tiles, :] = value.reshape(devices, tiles, LANES)
 
         correlate(
-            lambda q: x_ref[q, c],
-            store,
-            rows,
-            outer_ref,
-            inner_ref,
-            turn_ref,
-            high_ref,
-            low_ref,
-            prod_ref,
-        )
+            load, store, rows, outer_ref, inner_ref, turn_ref, high_ref, low_ref, prod_ref
+        )
+
+        @pl.loop(0, devices - 1)
+        def _(i):
+            returning(c, partner(i)).start()
+
+        at = pl.multiple_of((me * own + c) * 2 * tiles, 2 * tiles)
+        land[pl.ds(at, 2 * tiles), :] = back[c, me]
+
+    landed = land.at[pl.ds(0, (devices - 1) * own * 2 * tiles), :]
+    pltpu.make_async_copy(landed, landed, land_sem).wait()
+    for q, ref in enumerate((out0_ref, out1_ref)):
+        for j in range(tiles):
+            block = land[pl.ds(q * tiles + j, own * devices, stride=2 * tiles), :]
+            ref[j * LANES : (j + 1) * LANES, :] = block.T
+    sent = send.at[pl.ds(0, (devices - 1) * own * 3 * tiles), :]
+    pltpu.make_async_copy(sent, sent, send_sem).wait()
+    pltpu.make_async_copy(landed, landed, back_sem).wait()
 
 
 def shards(signal, filter_taps, grad_out):
     rows_local, channels = signal.shape
-    devices = lax.axis_size("gx") * lax.axis_size("gy")
+    columns = lax.axis_size("gy")
+    devices = lax.axis_size("gx") * columns
     tiles = rows_local // LANES
     rows = devices * tiles
     own = channels // devices
     outer, inner, turn = make_tables(rows)
-    x = jnp.stack([filter_taps, signal, grad_out])
-    x = x.reshape(3, tiles, LANES, channels).transpose(0, 3, 1, 2)
-    x = lax.all_to_all(x, ("gx", "gy"), split_axis=1, concat_axis=2, tiled=True)
     vmem = pl.BlockSpec(memory_space=pltpu.VMEM)
-    y = pl.pallas_call(
-        local_kernel,
-        out_shape=jax.ShapeDtypeStruct((2, own, rows, LANES), f32),
-        in_specs=[vmem] * 4,
-        out_specs=vmem,
+    anywhere = pl.BlockSpec(memory_space=pl.ANY)
+    result = jax.ShapeDtypeStruct((rows_local, channels), f32)
+    return pl.pallas_call(
+        functools.partial(kernel, columns),
+        out_shape=(result, result),
+        in_specs=[vmem] * 3 + [anywhere] * 3,
+        out_specs=(vmem, vmem),
         scratch_shapes=[
+            pltpu.VMEM((channels * 3 * tiles, LANES), f32),
+            pltpu.VMEM((own, devices, 3 * tiles, LANES), f32),
+            pltpu.VMEM((own, devices, 2 * tiles, LANES), f32),
+            pltpu.VMEM((channels * 2 * tiles, LANES), f32),
+            pltpu.VMEM(outer.shape, bf16),
+            pltpu.VMEM(inner.shape, bf16),
+            pltpu.VMEM(turn.shape, f32),
             pltpu.VMEM((rows, 6 * LANES), bf16),
             pltpu.VMEM((rows, 6 * LANES), bf16),
             pltpu.VMEM((2 * rows, 6 * LANES), f32),
+            pltpu.SemaphoreType.DMA((3,)),
+            pltpu.SemaphoreType.DMA,
+            pltpu.SemaphoreType.DMA((own,)),
+            pltpu.SemaphoreType.DMA,
+            pltpu.SemaphoreType.DMA,
         ],
-        compiler_params=pltpu.CompilerParams(vmem_limit_bytes=60 << 20),
-    )(x, outer, inner, turn)
-    y = lax.all_to_all(y, ("gx", "gy"), split_axis=2, concat_axis=1, tiled=True)
-    y = y.transpose(0, 2, 3, 1).reshape(2, rows_local, channels)
-    return y[0], y[1]
+        compiler_params=pltpu.CompilerParams(
+            collective_id=0, has_side_effects=True, vmem_limit_bytes=60 << 20
+        ),
+    )(signal, filter_taps, grad_out, outer, inner, turn)
 
 
 def solution(mesh):

time: 97.7 us -> 71.1 us (0.73)
  blocking collectives: 74.5 us -> 0 us
  Pallas kernels: 13.6 us -> 67.6 us
  local copies, waits for them, and re-layouts: 8.5 us -> 2.72 us
    all_to_all x2 -> x0, blocking collectives: 74.5 us -> none  [the longest x1 45.9 us: shards(): x = lax.all_to_all(x, ('gx', 'gy'), split_axis=1, concat_axis=2, tiled=True)]
    pallas_call x1, Pallas kernels: 13.6 us -> 67.6 us  [shards(): pl.pallas_call(functools.partial(kernel, columns), out_shape=(result, res...]
    another operation x3 -> x0, local copies, waits for them, and re-layouts: 2.84 us -> none  [shards(): x = jnp.stack([filter_taps, signal, grad_out])]
    pallas_call x1 -> x0, local copies, waits for them, and re-layouts: 1.9 us -> none  [shards(): pl.pallas_call(local_kernel, out_shape=jax.ShapeDtypeStruct((2, own, rows...]
    all_to_all x3 -> x0, local copies, waits for them, and re-layouts: 1.62 us -> none  [the longest x1 1.29 us: shards(): x = lax.all_to_all(x, ('gx', 'gy'), split_axis=1, concat_axis=2, tiled=True)]
where the time goes in v1:
time: 71.1 us; the launch traced here: 70.9 us
  Pallas kernels  67.6 us (95%)
  local copies, waits for them, and re-layouts  2.72 us (4%)
    pallas_call x1, Pallas kernels, shards(): pl.pallas_call(functools.partial(kernel, columns), out_shape=(result, res...  67.6 us
    unnamed x4, local copies, waits for them, and re-layouts  2.72 us

profile of v1, /device:TPU:0, one launch (start us, length us, event | category | flops | bytes accessed | tf_op | source)
XLA Modules:
  0.0 70.9 jit_solution(17880416220517726199)
XLA Ops:
  0.6 67.6 %shard_map.77 = (f32[1024,128]{1,0:T(8,128)}, f32[1024,128]{1,0:T(8,128)}) custom-call(f32[1024,128]{1,0:T(8,128)} %signal_ref.1, f32[1024,128]{1,0:T(8,128)} %filter_ref.1, f32[1024,128]{1,0:T(8,128)} %grad_ref.1, bf16[2,512,256]{2,1,0:T(8,128)(2,1)} %constant.6.clone.outer_hbm, bf16[2,256,256]{2,1,0:T(8,128)(2,1)} %constant.7.clone.inner_hbm, ...), custom_call_target="tpu_custom_call" | custom-call | tf_op jit(solution)/shard_map/pallas_call | solution.py:273
  68.2 0.0 copy-start
  68.2 1.9 %copy.10 = f32[1024,128]{1,0:T(8,128)} copy(f32[1024,128]{1,0:T(8,128)} %get-tuple-element.4) | data formatting | bytes 1048576
  70.1 0.0 copy-done
  70.2 0.8 %copy.11 = f32[1024,128]{1,0:T(8,128)} copy(f32[1024,128]{1,0:T(8,128)S(1)} %copy-done) | data formatting | bytes 1048576
Async XLA Ops:
  68.2 1.9 %copy-start = (f32[1024,128]{1,0:T(8,128)S(1)}, f32[1024,128]{1,0:T(8,128)}, u32[]{:S(2)}) copy-start(f32[1024,128]{1,0:T(8,128)} %get-tuple-element.5) | copy-start | bytes 1572868

commit v2 on v1

--- a/solution.py
+++ b/solution.py
@@ -133,29 +133,30 @@
 
 def kernel(
     columns,
-    signal_ref,
-    filter_ref,
-    grad_ref,
+    signal_hbm,
+    filter_hbm,
+    grad_hbm,
     outer_hbm,
     inner_hbm,
     turn_hbm,
-    out0_ref,
-    out1_ref,
+    land,
+    block_ref,
     send,
     recv,
     back,
-    land,
     outer_ref,
     inner_ref,
     turn_ref,
     high_ref,
     low_ref,
     prod_ref,
+    block_sem,
     table_sem,
     send_sem,
     recv_sem,
     back_sem,
     land_sem,
+    own_sem,
 ):
     own, devices, height, _ = recv.shape
     tiles = height // 3
@@ -166,8 +167,14 @@
         return (peer // columns, peer % columns)
 
     def partner(i):
-        return peer_of(me, devices - 1 - i, devices)
-
+        return peer_of(me, i + 1, devices)
+
+    blocks = [
+        pltpu.make_async_copy(ref, block_ref.at[q], block_sem.at[q])
+        for q, ref in enumerate((filter_hbm, signal_hbm, grad_hbm))
+    ]
+    for copy in blocks:
+        copy.start()
     barrier = pltpu.get_barrier_semaphore()
 
     @pl.loop(0, devices - 1)
@@ -184,9 +191,10 @@
     ]
     for copy in tables:
         copy.start()
-    for q, ref in enumerate((filter_ref, signal_ref, grad_ref)):
+    for q in range(3):
+        blocks[q].wait()
         for j in range(tiles):
-            block = ref[j * LANES : (j + 1) * LANES, :].T
+            block = block_ref[q, j * LANES : (j + 1) * LANES, :].T
             send[pl.ds(q * tiles + j, own * devices, stride=3 * tiles), :] = block
     pl.semaphore_wait(barrier, devices - 1)
 
@@ -212,6 +220,12 @@
             device_id_type=pl.DeviceIdType.MESH,
         )
 
+    def keep(c):
+        at = pl.multiple_of((me * own + c) * 2 * tiles, 2 * tiles)
+        return pltpu.make_async_copy(
+            back.at[c, me], land.at[pl.ds(at, 2 * tiles), :], own_sem.at[c]
+        )
+
     @pl.loop(0, own)
     def _(c):
         @pl.loop(0, devices - 1)
@@ -245,18 +259,27 @@
         def _(i):
             returning(c, partner(i)).start()
 
-        at = pl.multiple_of((me * own + c) * 2 * tiles, 2 * tiles)
-        land[pl.ds(at, 2 * tiles), :] = back[c, me]
+        keep(c).start()
 
     landed = land.at[pl.ds(0, (devices - 1) * own * 2 * tiles), :]
     pltpu.make_async_copy(landed, landed, land_sem).wait()
-    for q, ref in enumerate((out0_ref, out1_ref)):
-        for j in range(tiles):
-            block = land[pl.ds(q * tiles + j, own * devices, stride=2 * tiles), :]
-            ref[j * LANES : (j + 1) * LANES, :] = block.T
+
+    @pl.loop(0, own)
+    def _(c):
+        keep(c).wait()
+
     sent = send.at[pl.ds(0, (devices - 1) * own * 3 * tiles), :]
     pltpu.make_async_copy(sent, sent, send_sem).wait()
     pltpu.make_async_copy(landed, landed, back_sem).wait()
+
+
+def spread_kernel(land, out0_ref, out1_ref):
+    tiles = out0_ref.shape[0] // LANES
+    channels = out0_ref.shape[1]
+    for q, ref in enumerate((out0_ref, out1_ref)):
+        for j in range(tiles):
+            block = land[pl.ds(q * tiles + j, channels, stride=2 * tiles), :]
+            ref[j * LANES : (j + 1) * LANES, :] = block.T
 
 
 def shards(signal, filter_taps, grad_out):
@@ -270,16 +293,16 @@
     vmem = pl.BlockSpec(memory_space=pltpu.VMEM)
     anywhere = pl.BlockSpec(memory_space=pl.ANY)
     result = jax.ShapeDtypeStruct((rows_local, channels), f32)
-    return pl.pallas_call(
+    land = pl.pallas_call(
         functools.partial(kernel, columns),
-        out_shape=(result, result),
-        in_specs=[vmem] * 3 + [anywhere] * 3,
-        out_specs=(vmem, vmem),
+        out_shape=jax.ShapeDtypeStruct((channels * 2 * tiles, LANES), f32),
+        in_specs=[anywhere] * 6,
+        out_specs=anywhere,
         scratch_shapes=[
+            pltpu.VMEM((3, rows_local, channels), f32),
             pltpu.VMEM((channels * 3 * tiles, LANES), f32),
             pltpu.VMEM((own, devices, 3 * tiles, LANES), f32),
             pltpu.VMEM((own, devices, 2 * tiles, LANES), f32),
-            pltpu.VMEM((channels * 2 * tiles, LANES), f32),
             pltpu.VMEM(outer.shape, bf16),
             pltpu.VMEM(inner.shape, bf16),
             pltpu.VMEM(turn.shape, f32),
@@ -287,15 +310,24 @@
             pltpu.VMEM((rows, 6 * LANES), bf16),
             pltpu.VMEM((2 * rows, 6 * LANES), f32),
             pltpu.SemaphoreType.DMA((3,)),
+            pltpu.SemaphoreType.DMA((3,)),
             pltpu.SemaphoreType.DMA,
             pltpu.SemaphoreType.DMA((own,)),
             pltpu.SemaphoreType.DMA,
             pltpu.SemaphoreType.DMA,
+            pltpu.SemaphoreType.DMA((own,)),
         ],
         compiler_params=pltpu.CompilerParams(
             collective_id=0, has_side_effects=True, vmem_limit_bytes=60 << 20
         ),
     )(signal, filter_taps, grad_out, outer, inner, turn)
+    return pl.pallas_call(
+        spread_kernel,
+        out_shape=(result, result),
+        in_specs=[vmem],
+        out_specs=(vmem, vmem),
+        compiler_params=pltpu.CompilerParams(vmem_limit_bytes=60 << 20),
+    )(land)
 
 
 def solution(mesh):

time: 71.1 us -> 68.7 us (0.966)
  local copies, waits for them, and re-layouts: 2.72 us -> 0 us
    unnamed x4 -> x0, local copies, waits for them, and re-layouts: 2.72 us -> none
    pallas_call x1 -> x2, Pallas kernels: 67.6 us -> 67.9 us  [the longest x1 65.5 us: shards(): pl.pallas_call(functools.partial(kernel, columns), out_shape=jax.ShapeDty...]
where the time goes in v2:
time: 68.7 us; the launch traced here: 68.6 us
  Pallas kernels  67.9 us (99%)
    pallas_call x1, Pallas kernels, shards(): pl.pallas_call(functools.partial(kernel, columns), out_shape=jax.ShapeDty...  65.5 us
    pallas_call x1, Pallas kernels, shards(): pl.pallas_call(spread_kernel, out_shape=(result, result), in_specs=[vmem]...  2.49 us

profile of v2, /device:TPU:0, one launch (start us, length us, event | category | flops | bytes accessed | tf_op | source)
XLA Modules:
  0.0 68.6 jit_solution(3389396828687158487)
XLA Ops:
  0.6 65.5 %shard_map.77.land = f32[2048,128]{1,0:T(8,128)} custom-call(f32[1024,128]{1,0:T(8,128)} %signal_hbm.1, f32[1024,128]{1,0:T(8,128)} %filter_hbm.1, f32[1024,128]{1,0:T(8,128)} %grad_hbm.1, bf16[2,512,256]{2,1,0:T(8,128)(2,1)} %constant.6.clone.outer_hbm, bf16[2,256,256]{2,1,0:T(8,128)(2,1)} %constant.7.clone.inner_hbm, f32[2,512,128]{2,1,0:T(8,128)} %constant.8.clone.turn_hbm), custom_call_target="tpu_custom_call" | custom-call | tf_op jit(solution)/shard_map/pallas_call | solution.py:296
  66.1 2.5 %shard_map.78 = (f32[1024,128]{1,0:T(8,128)}, f32[1024,128]{1,0:T(8,128)}) custom-call(f32[2048,128]{1,0:T(8,128)} %shard_map.77.land), custom_call_target="tpu_custom_call" | custom-call | tf_op jit(solution)/shard_map/pallas_call | solution.py:324

commit v3 on v2

--- a/solution.py
+++ b/solution.py
@@ -180,7 +180,10 @@
     @pl.loop(0, devices - 1)
     def _(i):
         pl.semaphore_signal(
-            barrier, inc=1, device_id=device(partner(i)), device_id_type=pl.DeviceIdType.MESH
+            barrier,
+            inc=1,
+            device_id=device(partner(devices - 2 - i)),
+            device_id_type=pl.DeviceIdType.MESH,
         )
 
     tables = [
@@ -191,18 +194,16 @@
     ]
     for copy in tables:
         copy.start()
-    for q in range(3):
+    def turn_block(q):
         blocks[q].wait()
         for j in range(tiles):
             block = block_ref[q, j * LANES : (j + 1) * LANES, :].T
             send[pl.ds(q * tiles + j, own * devices, stride=3 * tiles), :] = block
-    pl.semaphore_wait(barrier, devices - 1)
-
-    def outgoing(c, peer):
-        at = pl.multiple_of((peer * own + c) * 3 * tiles, 3 * tiles)
+    def outgoing(c, peer, begin, end):
+        at = pl.multiple_of((peer * own + c) * 3 * tiles + begin * tiles, tiles)
         return pltpu.make_async_remote_copy(
-            src_ref=send.at[pl.ds(at, 3 * tiles), :],
-            dst_ref=recv.at[c, me],
+            src_ref=send.at[pl.ds(at, (end - begin) * tiles), :],
+            dst_ref=recv.at[c, me, begin * tiles : end * tiles, :],
             send_sem=send_sem,
             recv_sem=recv_sem.at[c],
             device_id=device(peer),
@@ -210,10 +211,10 @@
         )
 
     def returning(c, peer):
-        at = pl.multiple_of((me * own + c) * 2 * tiles, 2 * tiles)
+        at = pl.multiple_of((me * own + c) * tiles, tiles)
         return pltpu.make_async_remote_copy(
             src_ref=back.at[c, peer],
-            dst_ref=land.at[pl.ds(at, 2 * tiles), :],
+            dst_ref=land.at[:, pl.ds(at, tiles), :],
             send_sem=back_sem,
             recv_sem=land_sem,
             device_id=device(peer),
@@ -221,16 +222,30 @@
         )
 
     def keep(c):
-        at = pl.multiple_of((me * own + c) * 2 * tiles, 2 * tiles)
+        at = pl.multiple_of((me * own + c) * tiles, tiles)
         return pltpu.make_async_copy(
-            back.at[c, me], land.at[pl.ds(at, 2 * tiles), :], own_sem.at[c]
-        )
-
-    @pl.loop(0, own)
+            back.at[c, me], land.at[:, pl.ds(at, tiles), :], own_sem.at[c]
+        )
+
+    turn_block(0)
+    pl.semaphore_wait(barrier, devices - 1)
+
+    @pl.loop(0, devices - 1)
+    def _(i):
+        outgoing(0, partner(i), 0, 1).start()
+
+    turn_block(1)
+    turn_block(2)
+
+    @pl.loop(0, devices - 1)
+    def _(i):
+        outgoing(0, partner(i), 1, 3).start()
+
+    @pl.loop(1, own)
     def _(c):
         @pl.loop(0, devices - 1)
         def _(i):
-            outgoing(c, partner(i)).start()
+            outgoing(c, partner(i), 0, 3).start()
 
     @pl.loop(0, own)
     def _(c):
@@ -249,7 +264,7 @@
             return recv[c, :, q * tiles : (q + 1) * tiles, :].reshape(rows, LANES)
 
         def store(q, value):
-            back[c, :, q * tiles : (q + 1) * tiles, :] = value.reshape(devices, tiles, LANES)
+            back[c, :, q] = value.reshape(devices, tiles, LANES)
 
         correlate(
             load, store, rows, outer_ref, inner_ref, turn_ref, high_ref, low_ref, prod_ref
@@ -261,7 +276,7 @@
 
         keep(c).start()
 
-    landed = land.at[pl.ds(0, (devices - 1) * own * 2 * tiles), :]
+    landed = land.at[:, pl.ds(0, (devices - 1) * own * tiles), :]
     pltpu.make_async_copy(landed, landed, land_sem).wait()
 
     @pl.loop(0, own)
@@ -273,13 +288,31 @@
     pltpu.make_async_copy(landed, landed, back_sem).wait()
 
 
-def spread_kernel(land, out0_ref, out1_ref):
-    tiles = out0_ref.shape[0] // LANES
-    channels = out0_ref.shape[1]
+def spread_kernel(land, out0_ref, out1_ref, land_ref, result_ref, in_sem, out_sem):
+    _, rows_local, channels = result_ref.shape
+    tiles = rows_local // LANES
+    reads = [
+        pltpu.make_async_copy(land.at[q], land_ref.at[q], in_sem.at[q]) for q in range(2)
+    ]
+    for copy in reads:
+        copy.start()
+    writes = []
+    half = rows_local // 2
     for q, ref in enumerate((out0_ref, out1_ref)):
+        reads[q].wait()
         for j in range(tiles):
-            block = land[pl.ds(q * tiles + j, channels, stride=2 * tiles), :]
-            ref[j * LANES : (j + 1) * LANES, :] = block.T
+            block = land_ref[q, pl.ds(j, channels, stride=tiles), :]
+            result_ref[q, j * LANES : (j + 1) * LANES, :] = block.T
+            if (j + 1) % (tiles // 2) == 0:
+                at = slice((j + 1) * LANES - half, (j + 1) * LANES)
+                writes.append(
+                    pltpu.make_async_copy(
+                        result_ref.at[q, at, :], ref.at[at, :], out_sem.at[len(writes)]
+                    )
+                )
+                writes[-1].start()
+    for copy in writes:
+        copy.wait()
 
 
 def shards(signal, filter_taps, grad_out):
@@ -290,19 +323,18 @@
     rows = devices * tiles
     own = channels // devices
     outer, inner, turn = make_tables(rows)
-    vmem = pl.BlockSpec(memory_space=pltpu.VMEM)
     anywhere = pl.BlockSpec(memory_space=pl.ANY)
     result = jax.ShapeDtypeStruct((rows_local, channels), f32)
     land = pl.pallas_call(
         functools.partial(kernel, columns),
-        out_shape=jax.ShapeDtypeStruct((channels * 2 * tiles, LANES), f32),
+        out_shape=jax.ShapeDtypeStruct((2, channels * tiles, LANES), f32),
         in_specs=[anywhere] * 6,
         out_specs=anywhere,
         scratch_shapes=[
             pltpu.VMEM((3, rows_local, channels), f32),
             pltpu.VMEM((channels * 3 * tiles, LANES), f32),
             pltpu.VMEM((own, devices, 3 * tiles, LANES), f32),
-            pltpu.VMEM((own, devices, 2 * tiles, LANES), f32),
+            pltpu.VMEM((own, devices, 2, tiles, LANES), f32),
             pltpu.VMEM(outer.shape, bf16),
             pltpu.VMEM(inner.shape, bf16),
             pltpu.VMEM(turn.shape, f32),
@@ -324,8 +356,14 @@
     return pl.pallas_call(
         spread_kernel,
         out_shape=(result, result),
-        in_specs=[vmem],
-        out_specs=(vmem, vmem),
+        in_specs=[anywhere],
+        out_specs=(anywhere, anywhere),
+        scratch_shapes=[
+            pltpu.VMEM((2, channels * tiles, LANES), f32),
+            pltpu.VMEM((2, rows_local, channels), f32),
+            pltpu.SemaphoreType.DMA((2,)),
+            pltpu.SemaphoreType.DMA((4,)),
+        ],
         compiler_params=pltpu.CompilerParams(vmem_limit_bytes=60 << 20),
     )(land)
 

time: 68.7 us -> 68.1 us (level)
  no operation moved by 1% of the time
where the time goes in v3:
time: 68.1 us; the launch traced here: 67.9 us
  Pallas kernels  67.3 us (99%)
    pallas_call x1, Pallas kernels, shards(): pl.pallas_call(functools.partial(kernel, columns), out_shape=jax.ShapeDty...  65 us
    pallas_call x1, Pallas kernels, shards(): pl.pallas_call(spread_kernel, out_shape=(result, result), in_specs=[anywh...  2.22 us

profile of v3, /device:TPU:0, one launch (start us, length us, event | category | flops | bytes accessed | tf_op | source)
XLA Modules:
  0.0 67.9 jit_solution(15844296788212514849)
XLA Ops:
  0.6 65.0 %shard_map.77.land = f32[2,1024,128]{2,1,0:T(8,128)} custom-call(f32[1024,128]{1,0:T(8,128)} %signal_hbm.1, f32[1024,128]{1,0:T(8,128)} %filter_hbm.1, f32[1024,128]{1,0:T(8,128)} %grad_hbm.1, bf16[2,512,256]{2,1,0:T(8,128)(2,1)} %constant.6.clone.outer_hbm, bf16[2,256,256]{2,1,0:T(8,128)(2,1)} %constant.7.clone.inner_hbm, f32[2,512,128]{2,1,0:T(8,128)} %constant.8.clone.turn_hbm), custom_call_target="tpu_custom_call" | custom-call | tf_op jit(solution)/shard_map/pallas_call | solution.py:328
  65.7 2.2 %shard_map.78 = (f32[1024,128]{1,0:T(8,128)}, f32[1024,128]{1,0:T(8,128)}) custom-call(f32[2,1024,128]{2,1,0:T(8,128)} %shard_map.77.land), custom_call_target="tpu_custom_call" | custom-call | tf_op jit(solution)/shard_map/pallas_call | solution.py:356
